TPU v7x, 512 devices: a whole 4x4x16 slice. The times are simulated.
512 devices in a mesh: swath: 32 (over z, core), chan: 16 (over x, y).
Axes of the slice: x: 4, y: 4, z: 16, core: 2. Of those that a mesh axis runs over, the one named last changes fastest.
Arguments:
- grid_profiles: bfloat16 [32768, 256], P('swath'), may hold values from -6 to 6
- send_lists: int32 [32, 32, 128], P('swath'), may hold values from 0 to 1023
- counts: int32 [32, 32], P('swath'), may hold values from 1 to 128, as said below
- angle_index: int32 [128], replicated, may hold values from 0 to 7
- jacobian: bfloat16 [3, 256, 608], P(None, None, 'chan'), may hold values from -0.375 to 0.375
- observed: bfloat16 [608, 131072], P('chan', 'swath'), may hold values from -6 to 6
- kappa: float32 [2, 608], P(None, 'chan'), may hold values from 0.04 to 0.24
- factor: bfloat16 [608, 608], P('chan')
Outputs:
- weighted: float32 [608, 131072], P('chan', 'swath')
Inputs may be any that keep to these rules, and one draw needn't show every extreme that they name: `counts`: some receiver gets 128 live slots from every sender; every entry is at least one.
All inputs are finite; a program needn't handle non-finite values.
Results may differ from a plain program's by a relative error of at most 0.0029.
Values may be sent and summed in bfloat16 or wider, within the bound.
A program may use at most 64 MiB of HBM per device.

v0:
```python
import math
import jax
import jax.numpy as jnp
from jax import lax
from jax.sharding import PartitionSpec as P

XTRACK = 128
NANG = 8
SWEEPS = 3
max_zenith = math.pi / 3.0


def edge_lines(block, width):
    count = lax.axis_size("swath")
    forward = [(i, i + 1) for i in range(count - 1)]
    backward = [(target, source) for source, target in forward]
    low = lax.ppermute(block[:, -width:], "swath", forward)
    high = lax.ppermute(block[:, :width], "swath", backward)
    return jnp.concatenate([low, block, high], axis=1)


def diffuse_once(extended, along_rate, cross_rate):
    center = extended[:, 1:-1]
    along_sum = extended[:, 2:] + extended[:, :-2] - 2.0 * center
    side_pad = jnp.pad(center, ((0, 0), (0, 0), (1, 1)))
    cross_sum = side_pad[:, :, 2:] + side_pad[:, :, :-2] - 2.0 * center
    return center + along_rate * along_sum + cross_rate * cross_sum


def on_device(grid_profiles, send_lists, counts, angle_index, jacobian, observed, kappa, factor):
    members = lax.axis_size("chan")
    member = lax.axis_index("chan")
    swaths = lax.axis_size("swath")
    swath = lax.axis_index("swath")
    slots = send_lists.shape[2]
    share = slots // members
    own_chan = observed.shape[0]
    pixel_count = observed.shape[1]
    line_count = pixel_count // XTRACK
    depth = grid_profiles.shape[1]
    rows = lax.dynamic_slice_in_dim(send_lists[0], member * share, share, axis=1)
    slot = member * share + jnp.arange(share, dtype=jnp.int32)
    live_slot = slot[None, :] < counts[0][:, None]
    zero_value = jnp.zeros((), grid_profiles.dtype)
    outgoing = jnp.where(live_slot[:, :, None], grid_profiles[rows], zero_value)
    incoming = lax.all_to_all(outgoing, "swath", split_axis=0, concat_axis=0, tiled=True)
    gathered = lax.all_gather(incoming, "chan", axis=0, tiled=False)
    pixel_profiles = gathered.transpose(1, 0, 2, 3).reshape(pixel_count, depth)
    whole_factor = lax.all_gather(factor, "chan", axis=0, tiled=True)
    model = jnp.einsum("mkc,pk->mcp", jacobian, pixel_profiles, preferred_element_type=jnp.float32)
    zenith = angle_index.astype(jnp.float32) * (max_zenith / (NANG - 1))
    slant_path = 1.0 / jnp.cos(zenith) - 1.0
    model = model.reshape(3, own_chan, line_count, XTRACK)
    departure = observed.astype(jnp.float32).reshape(own_chan, line_count, XTRACK) - (
        model[0] + slant_path * model[1] + slant_path * slant_path * model[2]
    )
    along_rate = kappa[0][:, None, None]
    cross_rate = kappa[1][:, None, None]
    field = edge_lines(departure, SWEEPS)
    line = swath * line_count - SWEEPS + jnp.arange(line_count + 2 * SWEEPS, dtype=jnp.int32)
    inside = (line >= 0) & (line < swaths * line_count)
    for sweep in range(SWEEPS):
        field = diffuse_once(field, along_rate, cross_rate)
        kept = inside[sweep + 1 : inside.shape[0] - sweep - 1]
        field = jnp.where(kept[None, :, None], field, 0.0)
    smoothed = field.reshape(own_chan, pixel_count).astype(jnp.bfloat16)
    every_channel = lax.all_to_all(smoothed, "chan", split_axis=1, concat_axis=0, tiled=True)
    weighted = jnp.dot(whole_factor, every_channel, preferred_element_type=jnp.float32)
    return lax.all_to_all(weighted, "chan", split_axis=0, concat_axis=1, tiled=True)


def solution(mesh):
    in_specs = (
        P("swath", None),
        P("swath", None, None),
        P("swath", None),
        P(),
        P(None, None, "chan"),
        P("chan", "swath"),
        P(None, "chan"),
        P("chan", None),
    )
    out_specs = P("chan", "swath")
    return jax.shard_map(
        on_device, mesh=mesh, in_specs=in_specs, out_specs=out_specs, check_vma=False
    )
```

profile of v0, /device:TPU:96, one launch (start us, length us, event | category | flops | bytes accessed | tf_op | source)
XLA Modules:
  0.0 163.9 jit_solution(3897559961001162474)
XLA Ops:
  6.5 0.0 copy-start
  6.5 0.0 copy-start.1
  6.5 0.0 all-gather.4.cloned.1.call-start
  6.5 0.9 compare_select_fusion
  7.4 0.1 reshape.103
  7.5 0.1 copy-done
  7.6 0.0 copy-start.5
  7.6 0.0 copy-start.4
  7.6 1.1 gather_fusion
  8.7 0.7 broadcast_compare_fusion
  9.5 0.1 bitcast_select_fusion
  9.6 28.5 %all_to_all.40 = bf16[32,8,256]{2,1,0:T(8,128)(2,1)} all-to-all(bf16[32,8,256]{2,1,0:T(8,128)(2,1)S(1)} %bitcast_select_fusion), channel_id=1, replica_groups=mesh['swath'=32,'chan'=16] {'swath'}, dimensions={0} | all-to-all | bytes 262144 | tf_op jit(solution)/shard_map/all_to_all | solution.py:46
  38.1 0.0 all-gather.4.cloned.1.call-update
  38.1 0.0 copy-done.1
  38.2 0.1 copy.18
  38.3 0.0 copy-done.5
  38.4 0.0 copy-done.4
  38.4 54.3 %all-gather.4.cloned.1.call-done = bf16[512,8,256]{2,1,0:T(8,128)(2,1)} async-done(((bf16[32,8,256]{2,1,0:T(8,128)(2,1)}), bf16[512,8,256]{2,1,0:T(8,128)(2,1)}) %all-gather.4.cloned.1.call-update) | async-done | bytes 2097168 | tf_op jit(solution)/shard_map/all_gather | solution.py:47
  92.7 0.0 copy-start.2
  92.7 1.8 %copy.15 = bf16[32,16,8,256]{3,2,1,0:T(8,128)(2,1)S(1)} copy(bf16[32,16,8,256]{3,2,0,1:T(8,128)(2,1)} %bitcast.57) | data formatting | bytes 4194304 | tf_op jit(solution)/shard_map/transpose | solution.py:48
  94.6 0.0 copy-done.2
  94.6 0.8 convolution_bitcast_fusion
  95.4 0.2 fusion.29
  95.6 0.1 copy.19
  95.7 0.1 copy.20
  95.9 0.1 copy.21
  96.0 0.3 fusion.23
  96.3 1.9 %collective-permute-start = (f32[38,3,128]{2,1,0:T(4,128)S(1)}, f32[38,3,128]{2,1,0:T(4,128)S(1)}, u32[]{:S(2)}, u32[]{:S(2)}) collective-permute-start(f32[38,3,128]{2,1,0:T(4,128)S(1)} %get-tuple-element.10), channel_id=1, source_target_pairs={{0,16},{16,32},{32,48},{48,64},{64,80},{80,96},{96,112},{112,128},... | collective-permute-start | bytes 175112 | tf_op jit(solution)/shard_map/ppermute | solution.py:17
  98.2 3.6 %collective-permute-start.1 = (f32[38,3,128]{2,1,0:T(4,128)S(1)}, f32[38,3,128]{2,1,0:T(4,128)S(1)}, u32[]{:S(2)}, u32[]{:S(2)}) collective-permute-start(f32[38,3,128]{2,1,0:T(4,128)S(1)} %get-tuple-element.11), channel_id=1, source_target_pairs={{16,0},{32,16},{48,32},{64,48},{80,64},{96,80},{112,96},{128,112},... | collective-permute-start | bytes 175112 | tf_op jit(solution)/shard_map/ppermute | solution.py:18
  101.9 0.1 slice.80
  102.0 0.1 slice.79
  102.1 0.1 slice.78
  102.1 0.0 collective-permute-done
  102.1 1.8 %collective-permute-done.1 = f32[38,3,128]{2,1,0:T(4,128)S(1)} collective-permute-done((f32[38,3,128]{2,1,0:T(4,128)S(1)}, f32[38,3,128]{2,1,0:T(4,128)S(1)}, u32[]{:S(2)}, u32[]{:S(2)}) %collective-permute-start.1) | collective-permute-done | bytes 58400 | tf_op jit(solution)/shard_map/ppermute | solution.py:18
  103.9 0.1 pad_maximum_fusion
  104.0 0.1 slice.110
  104.1 0.7 fusion.4
  104.8 0.1 slice.113
  104.8 0.7 fusion.9
  105.5 0.1 slice.116
  105.6 0.0 copy-start.3
  105.6 0.7 fusion.21
  106.3 0.1 convert_element_type.19
  106.4 0.8 copy.16
  107.2 4.9 %all-to-all-start.1 = ((bf16[38,16,256]{2,0,1:T(8,128)(2,1)}), bf16[38,16,256]{2,0,1:T(8,128)(2,1)S(1)}, u32[]{:S(2)}, u32[]{:S(2)}) async-start(bf16[38,16,256]{2,0,1:T(8,128)(2,1)} %copy.16), calls=%async_computation.1 | async-start | bytes 655360 | tf_op jit(solution)/shard_map/all_to_all | solution.py:67
  112.1 0.0 copy-done.3
  112.2 25.8 %all-gather.1 = bf16[16,38,608]{2,1,0:T(8,128)(2,1)S(1)} all-gather(bf16[1,38,608]{2,1,0:T(8,128)(2,1)S(1)} %bitcast.59), channel_id=1, replica_groups=mesh['swath'=32,'chan'=16] {'chan'}, dimensions={0}, use_global_device_ids=true | all-gather | bytes 785536 | tf_op jit(solution)/shard_map/all_gather | solution.py:49
  137.9 0.4 reshape.112
  138.3 0.0 all-to-all-done.1
  138.3 0.1 all_to_all.32
  138.4 0.4 convolution_bitcast_fusion.1
  138.8 0.1 all_to_all.33
  138.9 16.7 %all_to_all.41 = f32[16,38,256]{2,1,0:T(8,128)S(1)} all-to-all(f32[16,38,256]{2,1,0:T(8,128)S(1)} %all_to_all.33), channel_id=1, replica_groups=mesh['swath'=32,'chan'=16] {'chan'}, dimensions={0} | all-to-all | bytes 1245184 | tf_op jit(solution)/shard_map/all_to_all | solution.py:69
  155.6 0.2 copy.17
  155.9 1.2 copy.22
  (8 shorter events, 0.2 us)
Async XLA Ops:
  6.5 1.1 copy-start
  6.5 31.6 %copy-start.1 = (bf16[38,4096]{1,0:T(8,128)(2,1)S(1)}, bf16[38,4096]{1,0:T(8,128)(2,1)}, u32[]{:S(2)}) copy-start(bf16[38,4096]{1,0:T(8,128)(2,1)} %param.13) | copy-start | bytes 933892
  6.5 86.2 %all-gather.4.cloned.1.call-start = ((), (), s32[]{:S(2)}) async-start(), calls=%async_computation.3 | async-start | bytes 2228224 | tf_op jit(solution)/shard_map/all_gather | solution.py:47
  7.6 30.7 %copy-start.5 = (s32[128]{0:T(128)S(1)}, s32[128]{0:T(128)}, u32[]{:S(2)}) copy-start(s32[128]{0:T(128)} %param.11) | copy-start | bytes 1540
  7.6 30.8 %copy-start.4 = (f32[2,38]{1,0:T(2,128)S(1)}, f32[2,38]{1,0:T(2,128)}, u32[]{:S(2)}) copy-start(f32[2,38]{1,0:T(2,128)} %param.14) | copy-start | bytes 916
  92.7 1.9 %copy-start.2 = (bf16[3,256,38]{1,2,0:T(8,128)(2,1)S(1)}, bf16[3,256,38]{1,2,0:T(8,128)(2,1)}, u32[]{:S(2)}) copy-start(bf16[3,256,38]{1,2,0:T(8,128)(2,1)} %param.12) | copy-start | bytes 175108
  96.3 5.8 %collective-permute-start = (f32[38,3,128]{2,1,0:T(4,128)S(1)}, f32[38,3,128]{2,1,0:T(4,128)S(1)}, u32[]{:S(2)}, u32[]{:S(2)}) collective-permute-start(f32[38,3,128]{2,1,0:T(4,128)S(1)} %get-tuple-element.10), channel_id=1, source_target_pairs={{0,16},{16,32},{32,48},{48,64},{64,80},{80,96},{96,112},{112,128},... | collective-permute-start | bytes 175112 | tf_op jit(solution)/shard_map/ppermute | solution.py:17
  98.2 5.6 %collective-permute-start.1 = (f32[38,3,128]{2,1,0:T(4,128)S(1)}, f32[38,3,128]{2,1,0:T(4,128)S(1)}, u32[]{:S(2)}, u32[]{:S(2)}) collective-permute-start(f32[38,3,128]{2,1,0:T(4,128)S(1)} %get-tuple-element.11), channel_id=1, source_target_pairs={{16,0},{32,16},{48,32},{64,48},{80,64},{96,80},{112,96},{128,112},... | collective-permute-start | bytes 175112 | tf_op jit(solution)/shard_map/ppermute | solution.py:18
  105.6 6.5 %copy-start.3 = (bf16[38,608]{1,0:T(8,128)(2,1)S(1)}, bf16[38,608]{1,0:T(8,128)(2,1)}, u32[]{:S(2)}) copy-start(bf16[38,608]{1,0:T(8,128)(2,1)} %param.15) | copy-start | bytes 138628
  107.2 31.1 %all-to-all-start.1 = ((bf16[38,16,256]{2,0,1:T(8,128)(2,1)}), bf16[38,16,256]{2,0,1:T(8,128)(2,1)S(1)}, u32[]{:S(2)}, u32[]{:S(2)}) async-start(bf16[38,16,256]{2,0,1:T(8,128)(2,1)} %copy.16), calls=%async_computation.1 | async-start | bytes 655360 | tf_op jit(solution)/shard_map/all_to_all | solution.py:67
Sparse Core Ops, SparseCore 0:
  38.2 54.4 all-gather.3
where the time goes:
time: 164 us
  blocking collectives  71 us (43%)
  waiting for transfers between devices  56.1 us (34%)
  between operations  13.7 us (8%)
  starting transfers between devices  10.5 us (6%)
  local copies, waits for them, and re-layouts  7.18 us (4%)
  other arithmetic  4.24 us (3%)
    all_gather x1, waiting for transfers between devices, on_device(): gathered = lax.all_gather(incoming, 'chan', axis=0, tiled=False)  54.3 us
    all_to_all x1, blocking collectives, on_device(): lax.all_to_all(outgoing, 'swath', split_axis=0, concat_axis=0, tiled=True)  28.5 us
    all_gather x1, blocking collectives, on_device(): whole_factor = lax.all_gather(factor, 'chan', axis=0, tiled=True)  25.8 us
    all_to_all x1, blocking collectives, on_device(): lax.all_to_all(weighted, 'chan', split_axis=0, concat_axis=1, tiled=True)  16.7 us
    all_to_all x1, starting transfers between devices, on_device(): lax.all_to_all(smoothed, 'chan', split_axis=1, concat_axis=0, tiled=True)  4.94 us
    ppermute x1, starting transfers between devices, edge_lines(): high = lax.ppermute(block[:, :width], 'swath', backward)  3.64 us
  transfers between devices with their start and end apart: 4, of which 2 were waited for; matrix products, arithmetic and copies ran while one was open for 0% of the time, Pallas kernels for 0%

commit v1 on v0

--- a/solution.py
+++ b/solution.py
@@ -66,7 +66,17 @@
     smoothed = field.reshape(own_chan, pixel_count).astype(jnp.bfloat16)
     every_channel = lax.all_to_all(smoothed, "chan", split_axis=1, concat_axis=0, tiled=True)
     weighted = jnp.dot(whole_factor, every_channel, preferred_element_type=jnp.float32)
-    return lax.all_to_all(weighted, "chan", split_axis=0, concat_axis=1, tiled=True)
+
+    def _launch_tables(chunk):
+        everything = jnp.concatenate(
+            lax.all_to_all(
+                jnp.stack(jnp.split(chunk, lax.axis_size("chan"), axis=0)), "chan", 0, 0
+            ),
+            axis=1,
+        )
+        return everything
+
+    return _launch_tables(weighted)
 
 
 def solution(mesh):

time: 164 us -> 164 us (level)
  no operation moved by 1% of the time
where the time goes in v1:
time: 164 us
  blocking collectives  71 us (43%)
  waiting for transfers between devices  56.1 us (34%)
  between operations  13.8 us (8%)
  starting transfers between devices  10.5 us (6%)
  local copies, waits for them, and re-layouts  7.21 us (4%)
  other arithmetic  4.24 us (3%)
    all_gather x1, waiting for transfers between devices, on_device(): gathered = lax.all_gather(incoming, 'chan', axis=0, tiled=False)  54.3 us
    all_to_all x1, blocking collectives, on_device(): lax.all_to_all(outgoing, 'swath', split_axis=0, concat_axis=0, tiled=True)  28.5 us
    all_gather x1, blocking collectives, on_device(): whole_factor = lax.all_gather(factor, 'chan', axis=0, tiled=True)  25.8 us
    all_to_all x1, blocking collectives, _launch_tables(): lax.all_to_all(jnp.stack(jnp.split(chunk, lax.axis_size('chan'), axis=0))...  16.7 us
    all_to_all x1, starting transfers between devices, on_device(): lax.all_to_all(smoothed, 'chan', split_axis=1, concat_axis=0, tiled=True)  4.94 us
    ppermute x1, starting transfers between devices, edge_lines(): high = lax.ppermute(block[:, :width], 'swath', backward)  3.64 us
  transfers between devices with their start and end apart: 4, of which 2 were waited for; matrix products, arithmetic and copies ran while one was open for 0% of the time, Pallas kernels for 0%

profile of v1, /device:TPU:96, one launch (start us, length us, event | category | flops | bytes accessed | tf_op | source)
XLA Modules:
  0.0 164.1 jit_solution(5391022183880514071)
XLA Ops:
  6.5 0.0 copy-start
  6.5 0.0 copy-start.1
  6.5 0.0 all-gather.4.cloned.1.call-start
  6.5 0.9 compare_select_fusion
  7.4 0.1 reshape.108
  7.5 0.1 copy-done
  7.6 0.0 copy-start.5
  7.6 0.0 copy-start.4
  7.6 1.1 gather_fusion
  8.7 0.7 broadcast_compare_fusion
  9.5 0.1 bitcast_select_fusion
  9.6 28.5 %all_to_all.26 = bf16[32,8,256]{2,1,0:T(8,128)(2,1)} all-to-all(bf16[32,8,256]{2,1,0:T(8,128)(2,1)S(1)} %bitcast_select_fusion), channel_id=1, replica_groups=mesh['swath'=32,'chan'=16] {'swath'}, dimensions={0} | all-to-all | bytes 262144 | tf_op jit(solution)/shard_map/all_to_all | solution.py:46
  38.1 0.0 all-gather.4.cloned.1.call-update
  38.1 0.0 copy-done.1
  38.2 0.1 copy.15
  38.3 0.0 copy-done.5
  38.4 0.0 copy-done.4
  38.4 54.3 %all-gather.4.cloned.1.call-done = bf16[512,8,256]{2,1,0:T(8,128)(2,1)} async-done(((bf16[32,8,256]{2,1,0:T(8,128)(2,1)}), bf16[512,8,256]{2,1,0:T(8,128)(2,1)}) %all-gather.4.cloned.1.call-update) | async-done | bytes 2097168 | tf_op jit(solution)/shard_map/all_gather | solution.py:47
  92.7 0.0 copy-start.2
  92.7 1.8 %copy.12 = bf16[32,16,8,256]{3,2,1,0:T(8,128)(2,1)S(1)} copy(bf16[32,16,8,256]{3,2,0,1:T(8,128)(2,1)} %bitcast.121) | data formatting | bytes 4194304 | tf_op jit(solution)/shard_map/transpose | solution.py:48
  94.6 0.0 copy-done.2
  94.6 0.8 convolution_bitcast_fusion
  95.4 0.2 fusion.45
  95.6 0.1 copy.16
  95.7 0.1 copy.17
  95.9 0.1 copy.18
  96.0 0.3 fusion.23
  96.3 1.9 %collective-permute-start = (f32[38,3,128]{2,1,0:T(4,128)S(1)}, f32[38,3,128]{2,1,0:T(4,128)S(1)}, u32[]{:S(2)}, u32[]{:S(2)}) collective-permute-start(f32[38,3,128]{2,1,0:T(4,128)S(1)} %get-tuple-element.10), channel_id=1, source_target_pairs={{0,16},{16,32},{32,48},{48,64},{64,80},{80,96},{96,112},{112,128},... | collective-permute-start | bytes 175112 | tf_op jit(solution)/shard_map/ppermute | solution.py:17
  98.2 3.6 %collective-permute-start.1 = (f32[38,3,128]{2,1,0:T(4,128)S(1)}, f32[38,3,128]{2,1,0:T(4,128)S(1)}, u32[]{:S(2)}, u32[]{:S(2)}) collective-permute-start(f32[38,3,128]{2,1,0:T(4,128)S(1)} %get-tuple-element.11), channel_id=1, source_target_pairs={{16,0},{32,16},{48,32},{64,48},{80,64},{96,80},{112,96},{128,112},... | collective-permute-start | bytes 175112 | tf_op jit(solution)/shard_map/ppermute | solution.py:18
  101.9 0.1 slice.80
  102.0 0.1 slice.79
  102.1 0.1 slice.78
  102.1 0.0 collective-permute-done
  102.1 1.8 %collective-permute-done.1 = f32[38,3,128]{2,1,0:T(4,128)S(1)} collective-permute-done((f32[38,3,128]{2,1,0:T(4,128)S(1)}, f32[38,3,128]{2,1,0:T(4,128)S(1)}, u32[]{:S(2)}, u32[]{:S(2)}) %collective-permute-start.1) | collective-permute-done | bytes 58400 | tf_op jit(solution)/shard_map/ppermute | solution.py:18
  103.9 0.1 pad_maximum_fusion
  104.0 0.1 slice.110
  104.1 0.7 fusion.4
  104.8 0.1 slice.113
  104.8 0.7 fusion.9
  105.5 0.1 slice.116
  105.6 0.0 copy-start.3
  105.6 0.7 fusion.21
  106.3 0.1 convert_element_type.19
  106.4 0.8 copy.13
  107.2 4.9 %all-to-all-start.1 = ((bf16[38,16,256]{2,0,1:T(8,128)(2,1)}), bf16[38,16,256]{2,0,1:T(8,128)(2,1)S(1)}, u32[]{:S(2)}, u32[]{:S(2)}) async-start(bf16[38,16,256]{2,0,1:T(8,128)(2,1)} %copy.13), calls=%async_computation.1 | async-start | bytes 655360 | tf_op jit(solution)/shard_map/all_to_all | solution.py:67
  112.1 0.0 copy-done.3
  112.2 25.8 %all-gather.1 = bf16[16,38,608]{2,1,0:T(8,128)(2,1)S(1)} all-gather(bf16[1,38,608]{2,1,0:T(8,128)(2,1)S(1)} %bitcast.123), channel_id=1, replica_groups=mesh['swath'=32,'chan'=16] {'chan'}, dimensions={0}, use_global_device_ids=true | all-gather | bytes 785536 | tf_op jit(solution)/shard_map/all_gather | solution.py:49
  137.9 0.4 reshape.117
  138.3 0.0 all-to-all-done.1
  138.3 0.1 all_to_all.21
  138.4 0.4 convolution_bitcast_fusion.1
  139.1 16.7 %all_to_all.27 = f32[16,38,256]{2,1,0:T(8,128)S(1)} all-to-all(f32[16,38,256]{2,1,0:T(8,128)S(1)} %fusion.28), channel_id=1, replica_groups=mesh['swath'=32,'chan'=16] {'chan'}, dimensions={0} | all-to-all | bytes 1245184 | tf_op jit(solution)/shard_map/all_to_all | solution.py:72
  155.8 0.2 copy.14
  156.0 1.2 copy.19
  (24 shorter events, 0.3 us)
Async XLA Ops:
  6.5 1.1 copy-start
  6.5 31.6 %copy-start.1 = (bf16[38,4096]{1,0:T(8,128)(2,1)S(1)}, bf16[38,4096]{1,0:T(8,128)(2,1)}, u32[]{:S(2)}) copy-start(bf16[38,4096]{1,0:T(8,128)(2,1)} %param.13) | copy-start | bytes 933892
  6.5 86.2 %all-gather.4.cloned.1.call-start = ((), (), s32[]{:S(2)}) async-start(), calls=%async_computation.3 | async-start | bytes 2228224 | tf_op jit(solution)/shard_map/all_gather | solution.py:47
  7.6 30.7 %copy-start.5 = (s32[128]{0:T(128)S(1)}, s32[128]{0:T(128)}, u32[]{:S(2)}) copy-start(s32[128]{0:T(128)} %param.11) | copy-start | bytes 1540
  7.6 30.8 %copy-start.4 = (f32[2,38]{1,0:T(2,128)S(1)}, f32[2,38]{1,0:T(2,128)}, u32[]{:S(2)}) copy-start(f32[2,38]{1,0:T(2,128)} %param.14) | copy-start | bytes 916
  92.7 1.9 %copy-start.2 = (bf16[3,256,38]{1,2,0:T(8,128)(2,1)S(1)}, bf16[3,256,38]{1,2,0:T(8,128)(2,1)}, u32[]{:S(2)}) copy-start(bf16[3,256,38]{1,2,0:T(8,128)(2,1)} %param.12) | copy-start | bytes 175108
  96.3 5.8 %collective-permute-start = (f32[38,3,128]{2,1,0:T(4,128)S(1)}, f32[38,3,128]{2,1,0:T(4,128)S(1)}, u32[]{:S(2)}, u32[]{:S(2)}) collective-permute-start(f32[38,3,128]{2,1,0:T(4,128)S(1)} %get-tuple-element.10), channel_id=1, source_target_pairs={{0,16},{16,32},{32,48},{48,64},{64,80},{80,96},{96,112},{112,128},... | collective-permute-start | bytes 175112 | tf_op jit(solution)/shard_map/ppermute | solution.py:17
  98.2 5.6 %collective-permute-start.1 = (f32[38,3,128]{2,1,0:T(4,128)S(1)}, f32[38,3,128]{2,1,0:T(4,128)S(1)}, u32[]{:S(2)}, u32[]{:S(2)}) collective-permute-start(f32[38,3,128]{2,1,0:T(4,128)S(1)} %get-tuple-element.11), channel_id=1, source_target_pairs={{16,0},{32,16},{48,32},{64,48},{80,64},{96,80},{112,96},{128,112},... | collective-permute-start | bytes 175112 | tf_op jit(solution)/shard_map/ppermute | solution.py:18
  105.6 6.5 %copy-start.3 = (bf16[38,608]{1,0:T(8,128)(2,1)S(1)}, bf16[38,608]{1,0:T(8,128)(2,1)}, u32[]{:S(2)}) copy-start(bf16[38,608]{1,0:T(8,128)(2,1)} %param.15) | copy-start | bytes 138628
  107.2 31.1 %all-to-all-start.1 = ((bf16[38,16,256]{2,0,1:T(8,128)(2,1)}), bf16[38,16,256]{2,0,1:T(8,128)(2,1)S(1)}, u32[]{:S(2)}, u32[]{:S(2)}) async-start(bf16[38,16,256]{2,0,1:T(8,128)(2,1)} %copy.13), calls=%async_computation.1 | async-start | bytes 655360 | tf_op jit(solution)/shard_map/all_to_all | solution.py:67
Sparse Core Ops, SparseCore 0:
  38.2 54.4 all-gather.3
